TPU v7x, 32 devices: a whole 2x2x4 slice. The times are simulated.
32 devices in a mesh: grp: 2 (over y), ctx: 4 (over z), head: 2 (over x), rep: 2 (over core).
Axes of the slice: x: 2, y: 2, z: 4, core: 2. Of those that a mesh axis runs over, the one named last changes fastest.
Arguments:
- queries: bfloat16 [8192, 2048], P(('grp', 'ctx', 'head', 'rep')), parts along dimension 0, may hold values from -10 to 10
- keys: bfloat16 [8192, 2048], P(('grp', 'ctx', 'head', 'rep')), parts along dimension 0, may hold values from -10 to 10
- values: bfloat16 [8192, 2048], P(('grp', 'ctx', 'head', 'rep')), parts along dimension 0, may hold values from -6 to 6
- reads: int32 [16, 8], P('grp'), parts along dimension 0, may hold values from 0 to 1, as said below
- owner: int32 [16], P('grp'), parts along dimension 0, may hold values from 0 to 7, as said below
Outputs:
- attended: bfloat16 [8192, 2048], P(('grp', 'ctx', 'head', 'rep')), parts along dimension 0
There are 2 independent parts, one for each index of `grp`. A program takes and returns all parts, laid end to end along the dimension named above; each array names one. Nothing has to cross between parts.
Inputs may be any that keep to these rules, and one draw needn't show every extreme that they name: `owner`: A permutation of the blocks in which sequence block b sits in slot b or in slot b with its lowest bit flipped. Every block reads itself; reads[kb, qb] is nonzero only where |kb - qb| <= 2 and |owner[kb] - owner[qb]| <= 3.
All inputs are finite; a program needn't handle non-finite values.
Results may differ from a plain program's by a relative error of at most 0.0047.
Values may be sent and summed in bfloat16 or wider, within the bound.
No kernel may reach another device: no remote copies, remote signals or barrier semaphores. Data moves between devices by JAX's collectives and lax.ppermute only.
A program may use at most 64 MiB of HBM per device.

v0:
```python
import math
import jax
import jax.numpy as jnp
from jax import lax
from jax.sharding import PartitionSpec as P

HEAD_DIM = 64
BLOCK = 512
REACH = 3


def from_behind(x, axis, by):
    devices = lax.axis_size(axis)
    pairs = [(i, i + by) for i in range(devices) if 0 <= i + by < devices]
    return lax.ppermute(x, axis, pairs)


def shards(queries, keys, values, reads, owner):
    query_heads, key_heads, value_heads = (
        lax.all_to_all(queries, ("head", "rep"), split_axis=1, concat_axis=0, tiled=True),
        lax.all_to_all(keys, ("head", "rep"), split_axis=1, concat_axis=0, tiled=True),
        lax.all_to_all(values, ("head", "rep"), split_axis=1, concat_axis=0, tiled=True),
    )
    row_count, feat_width = query_heads.shape
    heads_dev = feat_width // HEAD_DIM
    blk_dev = row_count // BLOCK
    reach_devs = -(-REACH // blk_dev)
    pair_kv = jnp.stack([key_heads, value_heads])
    lower_list = []
    upper_list = []
    moving = pair_kv
    for hop_index in range(reach_devs):
        moving = from_behind(moving, "ctx", 1)
        lower_list.insert(0, moving)
    moving = pair_kv
    for hop_index in range(reach_devs):
        moving = from_behind(moving, "ctx", -1)
        upper_list.append(moving)
    pieces = lower_list + [pair_kv] + upper_list
    window = jnp.concatenate(pieces, axis=1)
    highest = lax.Precision.HIGHEST
    block_count = reads.shape[0]
    slots = jnp.arange(block_count, dtype=jnp.int32)
    placed = (owner[:, None] == slots[None, :]).astype(jnp.float32)
    slot_reads = jnp.dot(
        jnp.dot(placed.T, reads.astype(jnp.float32), precision=highest), placed, precision=highest
    )
    padded_reads = jnp.pad(slot_reads, ((REACH, REACH), (0, 0)))
    ctx_index = lax.axis_index("ctx")
    scale_factor = 1.0 / math.sqrt(HEAD_DIM)
    tile_rows = min(512, BLOCK)
    tile_count = row_count // tile_rows

    def attend_tile(tile_id):
        local_block = tile_id * tile_rows // BLOCK
        query_slot = ctx_index * blk_dev + local_block
        column = lax.dynamic_index_in_dim(padded_reads, query_slot, 1, keepdims=False)
        allowed = lax.dynamic_slice_in_dim(column, query_slot, 2 * REACH + 1)
        query_tile = lax.dynamic_slice_in_dim(query_heads, tile_id * tile_rows, tile_rows, 0)
        query_tile = query_tile.reshape(tile_rows, heads_dev, HEAD_DIM)

        def key_block(relative):
            start = (reach_devs * blk_dev + local_block + relative) * BLOCK
            picked = lax.dynamic_slice_in_dim(window, start, BLOCK, 1)
            return picked.reshape(2, BLOCK, heads_dev, HEAD_DIM)

        def block_scores(kv_block):
            return (
                jnp.einsum(
                    "qhd,khd->hqk", query_tile, kv_block[0], preferred_element_type=jnp.float32
                )
                * scale_factor
            )

        def add_weights(pair, scores, value_block, row_max):
            weights = jnp.exp(scores - row_max[:, :, None])
            row_total = pair[1] + jnp.sum(weights, axis=-1)
            rounded = weights.astype(jnp.bfloat16)
            accum_out = pair[0] + jnp.einsum(
                "hqk,khd->qhd", rounded, value_block, preferred_element_type=jnp.float32
            )
            return (accum_out, row_total)

        row_max = jnp.full((heads_dev, tile_rows), -jnp.inf, jnp.float32)
        for position in range(2 * REACH + 1):
            is_read = allowed[position] > 0.5
            kv_block = key_block(position - REACH)
            row_max = lax.cond(
                is_read,
                lambda current, chosen=kv_block: jnp.maximum(
                    current, jnp.max(block_scores(chosen), axis=-1)
                ),
                lambda current: current,
                row_max,
            )
        totals = (
            jnp.zeros((tile_rows, heads_dev, HEAD_DIM), jnp.float32),
            jnp.zeros((heads_dev, tile_rows), jnp.float32),
        )
        for position in range(2 * REACH + 1):
            is_read = allowed[position] > 0.5
            kv_block = key_block(position - REACH)
            totals = lax.cond(
                is_read,
                lambda pair, chosen=kv_block: add_weights(
                    pair, block_scores(chosen), chosen[1], row_max
                ),
                lambda pair: pair,
                totals,
            )
        result = totals[0] / jnp.transpose(totals[1])[:, :, None]
        return result.reshape(tile_rows, feat_width).astype(jnp.bfloat16)

    tiles_out = lax.map(attend_tile, jnp.arange(tile_count, dtype=jnp.int32))
    attended = tiles_out.reshape(row_count, feat_width)
    return lax.all_to_all(attended, ("head", "rep"), split_axis=0, concat_axis=1, tiled=True)


def solution(mesh):
    placed = (
        P(("grp", "ctx", "head", "rep"), None),
        P(("grp", "ctx", "head", "rep"), None),
        P(("grp", "ctx", "head", "rep"), None),
        P("grp", None),
        P("grp"),
    )
    return jax.shard_map(
        shards,
        mesh=mesh,
        in_specs=placed,
        out_specs=P(("grp", "ctx", "head", "rep"), None),
        check_vma=False,
    )
```

profile of v0, /device:TPU:20, one launch (start us, length us, event | category | flops | bytes accessed | tf_op | source)
XLA Modules:
  0.0 273.8 jit_solution(7795582679675282533)
XLA Ops:
  0.0 2.3 copy.60
  2.3 3.5 %all-to-all-start = ((bf16[256,4,512]{0,2,1:T(8,128)(2,1)}), bf16[256,4,512]{0,2,1:T(8,128)(2,1)S(1)}, u32[]{:S(2)}, u32[]{:S(2)}) async-start(bf16[256,4,512]{0,2,1:T(8,128)(2,1)} %bitcast.46), calls=%async_computation | async-start | bytes 2097152 | tf_op jit(solution)/shard_map/all_to_all | solution.py:21
  5.8 2.3 copy.62
  8.1 12.1 %all-to-all-done = bf16[256,4,512]{0,2,1:T(8,128)(2,1)S(1)} async-done(((bf16[256,4,512]{0,2,1:T(8,128)(2,1)}), bf16[256,4,512]{0,2,1:T(8,128)(2,1)S(1)}, u32[]{:S(2)}, u32[]{:S(2)}) %all-to-all-start) | async-done | bytes 1048608 | tf_op jit(solution)/shard_map/all_to_all | solution.py:21
  20.2 3.5 %all-to-all-start.1 = ((bf16[256,4,512]{0,2,1:T(8,128)(2,1)}), bf16[256,4,512]{0,2,1:T(8,128)(2,1)S(1)}, u32[]{:S(2)}, u32[]{:S(2)}) async-start(bf16[256,4,512]{0,2,1:T(8,128)(2,1)} %bitcast.49), calls=%async_computation.1 | async-start | bytes 2097152 | tf_op jit(solution)/shard_map/all_to_all | solution.py:22
  24.3 13.8 %all-to-all-done.1 = bf16[256,4,512]{0,2,1:T(8,128)(2,1)S(1)} async-done(((bf16[256,4,512]{0,2,1:T(8,128)(2,1)}), bf16[256,4,512]{0,2,1:T(8,128)(2,1)S(1)}, u32[]{:S(2)}, u32[]{:S(2)}) %all-to-all-start.1) | async-done | bytes 1048608 | tf_op jit(solution)/shard_map/all_to_all | solution.py:22
  38.9 3.5 %collective-permute-start = (bf16[2,1024,512]{2,1,0:T(8,128)(2,1)S(1)}, bf16[2,1024,512]{2,1,0:T(8,128)(2,1)}, u32[]{:S(2)}, u32[]{:S(2)}) collective-permute-start(bf16[2,1024,512]{2,1,0:T(8,128)(2,1)S(1)} %pad_maximum_fusion), channel_id=1, source_target_pairs={{0,4},{4,8},{8,12},{1,5},{5,9},{9,13},{2,6},{6,10},{10,14},{3,7},{... | collective-permute-start | bytes 6291464 | tf_op jit(solution)/shard_map/ppermute | solution.py:15
  42.3 2.4 collective-permute-start.2
  44.7 43.2 %collective-permute-done = bf16[2,1024,512]{2,1,0:T(8,128)(2,1)} collective-permute-done((bf16[2,1024,512]{2,1,0:T(8,128)(2,1)S(1)}, bf16[2,1024,512]{2,1,0:T(8,128)(2,1)}, u32[]{:S(2)}, u32[]{:S(2)}) %collective-permute-start) | collective-permute-done | bytes 2097184 | tf_op jit(solution)/shard_map/ppermute | solution.py:15
  87.9 3.5 %collective-permute-start.1 = (bf16[2,1024,512]{2,1,0:T(8,128)(2,1)}, bf16[2,1024,512]{2,1,0:T(8,128)(2,1)}, u32[]{:S(2)}, u32[]{:S(2)}) collective-permute-start(bf16[2,1024,512]{2,1,0:T(8,128)(2,1)} %collective-permute-done), channel_id=1, source_target_pairs={{0,4},{4,8},{8,12},{1,5},{5,9},{9,13},{2,6},{6,10},{10,14},{3,7},{... | collective-permute-start | bytes 6291464 | tf_op jit(solution)/shard_map/ppermute | solution.py:15
  91.4 2.4 collective-permute-start.3
  93.8 2.3 copy.64
  96.1 3.5 %all-to-all-start.2 = ((bf16[256,4,512]{0,2,1:T(8,128)(2,1)}), bf16[256,4,512]{0,2,1:T(8,128)(2,1)S(1)}, u32[]{:S(2)}, u32[]{:S(2)}) async-start(bf16[256,4,512]{0,2,1:T(8,128)(2,1)} %bitcast.222), calls=%async_computation.2 | async-start | bytes 2097152 | tf_op jit(solution)/shard_map/all_to_all | solution.py:20
  100.2 13.8 %all-to-all-done.2 = bf16[256,4,512]{0,2,1:T(8,128)(2,1)S(1)} async-done(((bf16[256,4,512]{0,2,1:T(8,128)(2,1)}), bf16[256,4,512]{0,2,1:T(8,128)(2,1)S(1)}, u32[]{:S(2)}, u32[]{:S(2)}) %all-to-all-start.2) | async-done | bytes 1048608 | tf_op jit(solution)/shard_map/all_to_all | solution.py:20
  115.3 21.0 %collective-permute-done.1 = bf16[2,1024,512]{2,1,0:T(8,128)(2,1)} collective-permute-done((bf16[2,1024,512]{2,1,0:T(8,128)(2,1)}, bf16[2,1024,512]{2,1,0:T(8,128)(2,1)}, u32[]{:S(2)}, u32[]{:S(2)}) %collective-permute-start.1) | collective-permute-done | bytes 2097184 | tf_op jit(solution)/shard_map/ppermute | solution.py:15
  136.3 3.1 %constant_dynamic-update-slice_fusion.5 = bf16[2,5120,512]{2,1,0:T(8,128)(2,1)} fusion(bf16[2,1024,512]{2,1,0:T(8,128)(2,1)} %collective-permute-done.1), kind=kLoop, calls=%fused_computation.133 | loop fusion | bytes 4194304
  139.4 3.1 %constant_dynamic-update-slice_fusion.4 = bf16[2,5120,512]{2,1,0:T(8,128)(2,1)} fusion(bf16[2,5120,512]{2,1,0:T(8,128)(2,1)} %constant_dynamic-update-slice_fusion.5, bf16[2,1024,512]{2,1,0:T(8,128)(2,1)} %collective-permute-done), kind=kLoop, calls=%fused_computation.132 | loop fusion | bytes 4194304
  144.0 3.0 %constant_dynamic-update-slice_fusion.2 = bf16[2,5120,512]{2,1,0:T(8,128)(2,1)} fusion(bf16[2,5120,512]{2,1,0:T(8,128)(2,1)} %constant_dynamic-update-slice_fusion.3, bf16[2,1024,512]{2,1,0:T(8,128)(2,1)} %collective-permute-done.2), kind=kLoop, calls=%fused_computation.130 | loop fusion | bytes 4194304
  147.0 3.1 %constant_dynamic-update-slice_fusion.1 = bf16[2,5120,512]{2,1,0:T(8,128)(2,1)} fusion(bf16[2,5120,512]{2,1,0:T(8,128)(2,1)} %constant_dynamic-update-slice_fusion.2, bf16[2,1024,512]{2,1,0:T(8,128)(2,1)} %collective-permute-done.3), kind=kLoop, calls=%fused_computation.129 | loop fusion | bytes 4194304 | tf_op jit(solution)/shard_map/concatenate | solution.py:40
  150.1 13.8 %copy.66 = bf16[2,5120,512]{1,2,0:T(8,128)(2,1)} copy(bf16[2,5120,512]{2,1,0:T(8,128)(2,1)} %constant_dynamic-update-slice_fusion.1) | data formatting | bytes 20971520 | tf_op jit(solution)/shard_map/while | solution.py:114
  163.9 90.1 %while.13 = (s32[]{:T(128)}, bf16[2,512,512]{2,1,0:T(8,128)(2,1)}, s32[2]{0:T(128)S(1)}, s32[]{:T(128)}, f32[14,8]{0,1:T(8,128)S(1)}, /*index=5*/bf16[2,5120,512...) while((s32[]{:T(128)}, bf16[2,512,512]{2,1,0:T(8,128)(2,1)}, ...), condition=%wide.region_43.44_spmd, body=%wide.region_0.43_spmd.sunk | while | flops 5756674048 | bytes 200296880 | solution.py:114
  165.2 5.5 %constant_dynamic-slice_fusion.10 = (bf16[2,512,512]{1,2,0:T(8,128)(2,1)S(1)}, bf16[2,512,512]{1,2,0:T(8,128)(2,1)}, bf16[2,512,512]{1,2,0:T(8,128)(2,1)}, bf16[...) fusion(bf16[2,5120,512]{1,2,0:T(8,128)(2,1)} %get-tuple-element, ...), kind=kLoop, calls=%fused_computation.120.clone.1 | loop fusion | bytes 14680092 | tf_op jit(solution)/shard_map/while/body/eval_jaxpr/dynamic_slice | solution.py:64
  174.5 2.4 conditional.29
  174.5 2.3 multiply_reduce_fusion.1
  178.0 2.4 conditional.31
  178.0 2.3 multiply_reduce_fusion.3
  181.1 2.4 conditional.32
  181.1 2.3 multiply_reduce_fusion.4
  184.1 2.4 conditional.33
  184.1 2.3 multiply_reduce_fusion.5
  188.6 4.8 %conditional.36 = ((f32[512,8,64]{0,2,1:T(8,128)S(1)}, f32[8,512]{1,0:T(8,128)S(1)})) conditional(s32[]{:T(128)} %bitcast.175, (f32[512,8,64]{0,2,1:T(8,128)S(1)}, f32[8,512]{1,0:T(8,128)S(1)}) %conditional.35, (bf16[2,512,8,64]{1,3,2,0:T(8,128)(2,1)}, bf16[512,8,64]{0,2,1:T(8,128)(2,1)S(1)}, f32[8,512]{1,0:T(8,128)S(1)}, ...), branch_computations={%region_25.25_spmd, %region_26.27_spmd} | conditional | flops 549715968 | bytes 24739892 | solution.py:103
  188.6 3.0 %fusion.29 = (f32[8,512]{1,0:T(8,128)S(1)}, f32[8,512,512]{1,2,0:T(8,128)S(1)}) fusion(f32[8,512]{1,0:T(8,128)S(1)} %get-tuple-element.344, bf16[512,8,64]{0,2,1:T(8,128)(2,1)S(1)} %get-tuple-element.342, bf16[2,512,8,64]{1,3,2,0:T(8,128)(2,1)} %get-tuple-element.343), kind=kOutput, calls=%fused_computation.35 | convolution fusion | flops 274722816 | bytes 9469952 | tf_op jit(solution)/shard_map/while/body/eval_jaxpr/cond/branch_1_fun/qhd,khd->hqk/dot_general | solution.py:69
  191.6 1.8 fusion.38
  193.5 4.8 %conditional.38 = ((f32[512,8,64]{0,2,1:T(8,128)S(1)}, f32[8,512]{1,0:T(8,128)S(1)})) conditional(s32[]{:T(128)} %bitcast.173, (f32[512,8,64]{0,2,1:T(8,128)S(1)}, f32[8,512]{1,0:T(8,128)S(1)}) %get-tuple-element.654, (bf16[2,512,8,64]{1,3,2,0:T(8,128)(2,1)}, bf16[512,8,64]{0,2,1:T(8,128)(2,1)S(1)}, f32[8,512]{1,0:T(8,128)S(1)}, ...), branch_computations={%region_31.31_spmd, %region_32.33_spmd} | conditional | flops 549715968 | bytes 24739892 | solution.py:103
  193.5 3.0 %fusion.65 = (f32[8,512]{1,0:T(8,128)S(1)}, f32[8,512,512]{1,2,0:T(8,128)S(1)}) fusion(f32[8,512]{1,0:T(8,128)S(1)} %get-tuple-element.354, bf16[512,8,64]{0,2,1:T(8,128)(2,1)S(1)} %get-tuple-element.352, bf16[2,512,8,64]{1,3,2,0:T(8,128)(2,1)} %get-tuple-element.353), kind=kOutput, calls=%fused_computation.63 | convolution fusion | flops 274722816 | bytes 9469952 | tf_op jit(solution)/shard_map/while/body/eval_jaxpr/cond/branch_1_fun/qhd,khd->hqk/dot_general | solution.py:69
  196.5 1.8 fusion.74
  198.3 3.9 %conditional.39 = ((f32[512,8,64]{0,2,1:T(8,128)S(1)}, f32[8,512]{1,0:T(8,128)S(1)})) conditional(s32[]{:T(128)} %bitcast.172, (f32[512,8,64]{0,2,1:T(8,128)S(1)}, f32[8,512]{1,0:T(8,128)S(1)}) %get-tuple-element.655, (bf16[2,512,8,64]{1,3,2,0:T(8,128)(2,1)S(1)}, bf16[512,8,64]{0,2,1:T(8,128)(2,1)S(1)}, f32[8,512]{1,0:T(8,128)S(1)}, ...), branch_computations={%region_34.34_spmd, %region_35.36_spmd} | conditional | flops 549715968 | bytes 20545560 | solution.py:103
  198.3 2.0 fusion.83
  200.4 1.8 fusion.92
  202.2 4.8 %conditional.40 = ((f32[512,8,64]{0,2,1:T(8,128)S(1)}, f32[8,512]{1,0:T(8,128)S(1)})) conditional(s32[]{:T(128)} %bitcast.171, (f32[512,8,64]{0,2,1:T(8,128)S(1)}, f32[8,512]{1,0:T(8,128)S(1)}) %get-tuple-element.656, (bf16[2,512,8,64]{1,3,2,0:T(8,128)(2,1)}, bf16[512,8,64]{0,2,1:T(8,128)(2,1)S(1)}, f32[8,512]{1,0:T(8,128)S(1)}, ...), branch_computations={%region_37.37_spmd, %region_38.39_spmd} | conditional | flops 549715968 | bytes 24739892 | solution.py:103
  202.2 3.0 %fusion.101 = (f32[8,512]{1,0:T(8,128)S(1)}, f32[8,512,512]{1,2,0:T(8,128)S(1)}) fusion(f32[8,512]{1,0:T(8,128)S(1)} %get-tuple-element.364, bf16[512,8,64]{0,2,1:T(8,128)(2,1)S(1)} %get-tuple-element.362, bf16[2,512,8,64]{1,3,2,0:T(8,128)(2,1)} %get-tuple-element.363), kind=kOutput, calls=%fused_computation.91 | convolution fusion | flops 274722816 | bytes 9469952 | tf_op jit(solution)/shard_map/while/body/eval_jaxpr/cond/branch_1_fun/qhd,khd->hqk/dot_general | solution.py:69
  205.2 1.8 fusion.110
  207.0 3.9 %conditional.41 = ((f32[512,8,64]{0,2,1:T(8,128)S(1)}, f32[8,512]{1,0:T(8,128)S(1)})) conditional(s32[]{:T(128)} %bitcast.170, (f32[512,8,64]{0,2,1:T(8,128)S(1)}, f32[8,512]{1,0:T(8,128)S(1)}) %get-tuple-element.657, (bf16[2,512,8,64]{1,3,2,0:T(8,128)(2,1)S(1)}, bf16[512,8,64]{0,2,1:T(8,128)(2,1)S(1)}, f32[8,512]{1,0:T(8,128)S(1)}, ...), branch_computations={%region_40.40_spmd, %region_41.42_spmd} | conditional | flops 549715968 | bytes 20545560 | solution.py:103
  207.1 2.0 fusion.119
  209.1 1.8 fusion.128
  213.4 5.5 %constant_dynamic-slice_fusion.10 = (bf16[2,512,512]{1,2,0:T(8,128)(2,1)S(1)}, bf16[2,512,512]{1,2,0:T(8,128)(2,1)}, bf16[2,512,512]{1,2,0:T(8,128)(2,1)}, bf16[...) fusion(bf16[2,5120,512]{1,2,0:T(8,128)(2,1)} %get-tuple-element, ...), kind=kLoop, calls=%fused_computation.120.clone.1 | loop fusion | bytes 14680092 | tf_op jit(solution)/shard_map/while/body/eval_jaxpr/dynamic_slice | solution.py:64
  224.0 2.4 conditional.29
  224.0 2.3 multiply_reduce_fusion.1
  227.0 2.4 conditional.30
  227.0 2.3 multiply_reduce_fusion.2
  229.9 2.4 conditional.31
  229.9 2.3 multiply_reduce_fusion.3
  234.3 3.6 %conditional.35 = (f32[512,8,64]{0,2,1:T(8,128)S(1)}, f32[8,512]{1,0:T(8,128)S(1)}) conditional(s32[]{:T(128)} %bitcast.176, () %tuple.155, (bf16[2,512,8,64]{1,3,2,0:T(8,128)(2,1)S(1)}, bf16[512,8,64]{0,2,1:T(8,128)(2,1)S(1)}, f32[8,512]{1,0:T(8,128)S(1)}) %tuple.229), branch_computations={%region_22.22_spmd, %region_23.24_spmd} | conditional | flops 549449728 | bytes 19447824 | solution.py:103
  234.3 2.0 fusion.14
  237.9 4.8 %conditional.36 = ((f32[512,8,64]{0,2,1:T(8,128)S(1)}, f32[8,512]{1,0:T(8,128)S(1)})) conditional(s32[]{:T(128)} %bitcast.175, (f32[512,8,64]{0,2,1:T(8,128)S(1)}, f32[8,512]{1,0:T(8,128)S(1)}) %conditional.35, (bf16[2,512,8,64]{1,3,2,0:T(8,128)(2,1)}, bf16[512,8,64]{0,2,1:T(8,128)(2,1)S(1)}, f32[8,512]{1,0:T(8,128)S(1)}, ...), branch_computations={%region_25.25_spmd, %region_26.27_spmd} | conditional | flops 549715968 | bytes 24739892 | solution.py:103
  237.9 3.0 %fusion.29 = (f32[8,512]{1,0:T(8,128)S(1)}, f32[8,512,512]{1,2,0:T(8,128)S(1)}) fusion(f32[8,512]{1,0:T(8,128)S(1)} %get-tuple-element.344, bf16[512,8,64]{0,2,1:T(8,128)(2,1)S(1)} %get-tuple-element.342, bf16[2,512,8,64]{1,3,2,0:T(8,128)(2,1)} %get-tuple-element.343), kind=kOutput, calls=%fused_computation.35 | convolution fusion | flops 274722816 | bytes 9469952 | tf_op jit(solution)/shard_map/while/body/eval_jaxpr/cond/branch_1_fun/qhd,khd->hqk/dot_general | solution.py:69
  241.0 1.8 fusion.38
  242.8 3.9 %conditional.37 = ((f32[512,8,64]{0,2,1:T(8,128)S(1)}, f32[8,512]{1,0:T(8,128)S(1)})) conditional(s32[]{:T(128)} %bitcast.174, (f32[512,8,64]{0,2,1:T(8,128)S(1)}, f32[8,512]{1,0:T(8,128)S(1)}) %get-tuple-element.653, (bf16[2,512,8,64]{1,3,2,0:T(8,128)(2,1)S(1)}, bf16[512,8,64]{0,2,1:T(8,128)(2,1)S(1)}, f32[8,512]{1,0:T(8,128)S(1)}, ...), branch_computations={%region_28.28_spmd, %region_29.30_spmd} | conditional | flops 549715968 | bytes 20545560 | solution.py:103
  242.8 2.0 fusion.47
  244.8 1.8 fusion.56
  246.6 4.8 %conditional.38 = ((f32[512,8,64]{0,2,1:T(8,128)S(1)}, f32[8,512]{1,0:T(8,128)S(1)})) conditional(s32[]{:T(128)} %bitcast.173, (f32[512,8,64]{0,2,1:T(8,128)S(1)}, f32[8,512]{1,0:T(8,128)S(1)}) %get-tuple-element.654, (bf16[2,512,8,64]{1,3,2,0:T(8,128)(2,1)}, bf16[512,8,64]{0,2,1:T(8,128)(2,1)S(1)}, f32[8,512]{1,0:T(8,128)S(1)}, ...), branch_computations={%region_31.31_spmd, %region_32.33_spmd} | conditional | flops 549715968 | bytes 24739892 | solution.py:103
  246.7 3.0 %fusion.65 = (f32[8,512]{1,0:T(8,128)S(1)}, f32[8,512,512]{1,2,0:T(8,128)S(1)}) fusion(f32[8,512]{1,0:T(8,128)S(1)} %get-tuple-element.354, bf16[512,8,64]{0,2,1:T(8,128)(2,1)S(1)} %get-tuple-element.352, bf16[2,512,8,64]{1,3,2,0:T(8,128)(2,1)} %get-tuple-element.353), kind=kOutput, calls=%fused_computation.63 | convolution fusion | flops 274722816 | bytes 9469952 | tf_op jit(solution)/shard_map/while/body/eval_jaxpr/cond/branch_1_fun/qhd,khd->hqk/dot_general | solution.py:69
  249.7 1.8 fusion.74
  253.9 17.9 %all_to_all.70 = bf16[4,256,512]{2,1,0:T(8,128)(2,1)S(1)} all-to-all(bf16[4,256,512]{2,1,0:T(8,128)(2,1)} %bitcast.225), channel_id=1, replica_groups=mesh['grp'=2,'ctx'=4,'head'=2,'rep'=2] {'head','rep'}, dimensions={0} | all-to-all | bytes 2097152 | tf_op jit(solution)/shard_map/all_to_all | solution.py:116
  (94 shorter events, 23.5 us)
Async XLA Ops:
  2.3 17.9 %all-to-all-start = ((bf16[256,4,512]{0,2,1:T(8,128)(2,1)}), bf16[256,4,512]{0,2,1:T(8,128)(2,1)S(1)}, u32[]{:S(2)}, u32[]{:S(2)}) async-start(bf16[256,4,512]{0,2,1:T(8,128)(2,1)} %bitcast.46), calls=%async_computation | async-start | bytes 2097152 | tf_op jit(solution)/shard_map/all_to_all | solution.py:21
  5.8 93.9 %copy-start.7 = (s32[8,8]{1,0:T(8,128)S(1)}, s32[8,8]{1,0:T(8,128)}, u32[]{:S(2)}) copy-start(s32[8,8]{1,0:T(8,128)} %param.38) | copy-start | bytes 772
  5.8 93.9 %copy-start.8 = (s32[8]{0:T(128)S(1)}, s32[8]{0:T(128)}, u32[]{:S(2)}) copy-start(s32[8]{0:T(128)} %param.39) | copy-start | bytes 100
  20.2 17.9 %all-to-all-start.1 = ((bf16[256,4,512]{0,2,1:T(8,128)(2,1)}), bf16[256,4,512]{0,2,1:T(8,128)(2,1)S(1)}, u32[]{:S(2)}, u32[]{:S(2)}) async-start(bf16[256,4,512]{0,2,1:T(8,128)(2,1)} %bitcast.49), calls=%async_computation.1 | async-start | bytes 2097152 | tf_op jit(solution)/shard_map/all_to_all | solution.py:22
  38.9 49.1 %collective-permute-start = (bf16[2,1024,512]{2,1,0:T(8,128)(2,1)S(1)}, bf16[2,1024,512]{2,1,0:T(8,128)(2,1)}, u32[]{:S(2)}, u32[]{:S(2)}) collective-permute-start(bf16[2,1024,512]{2,1,0:T(8,128)(2,1)S(1)} %pad_maximum_fusion), channel_id=1, source_target_pairs={{0,4},{4,8},{8,12},{1,5},{5,9},{9,13},{2,6},{6,10},{10,14},{3,7},{... | collective-permute-start | bytes 6291464 | tf_op jit(solution)/shard_map/ppermute | solution.py:15
  42.3 49.1 %collective-permute-start.2 = (bf16[2,1024,512]{2,1,0:T(8,128)(2,1)S(1)}, bf16[2,1024,512]{2,1,0:T(8,128)(2,1)}, u32[]{:S(2)}, u32[]{:S(2)}) collective-permute-start(bf16[2,1024,512]{2,1,0:T(8,128)(2,1)S(1)} %pad_maximum_fusion), channel_id=1, source_target_pairs={{4,0},{8,4},{12,8},{5,1},{9,5},{13,9},{6,2},{10,6},{14,10},{7,3},{... | collective-permute-start | bytes 6291464 | tf_op jit(solution)/shard_map/ppermute | solution.py:15
  87.9 48.4 %collective-permute-start.1 = (bf16[2,1024,512]{2,1,0:T(8,128)(2,1)}, bf16[2,1024,512]{2,1,0:T(8,128)(2,1)}, u32[]{:S(2)}, u32[]{:S(2)}) collective-permute-start(bf16[2,1024,512]{2,1,0:T(8,128)(2,1)} %collective-permute-done), channel_id=1, source_target_pairs={{0,4},{4,8},{8,12},{1,5},{5,9},{9,13},{2,6},{6,10},{10,14},{3,7},{... | collective-permute-start | bytes 6291464 | tf_op jit(solution)/shard_map/ppermute | solution.py:15
  91.4 55.6 %collective-permute-start.3 = (bf16[2,1024,512]{2,1,0:T(8,128)(2,1)}, bf16[2,1024,512]{2,1,0:T(8,128)(2,1)}, u32[]{:S(2)}, u32[]{:S(2)}) collective-permute-start(bf16[2,1024,512]{2,1,0:T(8,128)(2,1)} %collective-permute-done.2), channel_id=1, source_target_pairs={{4,0},{8,4},{12,8},{5,1},{9,5},{13,9},{6,2},{10,6},{14,10},{7,3},{... | collective-permute-start | bytes 6291464 | tf_op jit(solution)/shard_map/ppermute | solution.py:15
  96.1 17.9 %all-to-all-start.2 = ((bf16[256,4,512]{0,2,1:T(8,128)(2,1)}), bf16[256,4,512]{0,2,1:T(8,128)(2,1)S(1)}, u32[]{:S(2)}, u32[]{:S(2)}) async-start(bf16[256,4,512]{0,2,1:T(8,128)(2,1)} %bitcast.222), calls=%async_computation.2 | async-start | bytes 2097152 | tf_op jit(solution)/shard_map/all_to_all | solution.py:20
  170.7 16.3 %copy-start = (bf16[2,512,512]{1,2,0:T(8,128)(2,1)}, bf16[2,512,512]{1,2,0:T(8,128)(2,1)S(1)}, u32[]{:S(2)}) copy-start(bf16[2,512,512]{1,2,0:T(8,128)(2,1)S(1)} %get-tuple-element.528) | copy-start | bytes 3145732 | tf_op jit(solution)/shard_map/while
  188.6 4.9 %copy-start.5 = (bf16[2,512,512]{1,2,0:T(8,128)(2,1)S(1)}, bf16[2,512,512]{1,2,0:T(8,128)(2,1)}, u32[]{:S(2)}) copy-start(bf16[2,512,512]{1,2,0:T(8,128)(2,1)} %get-tuple-element.524) | copy-start | bytes 3145732 | tf_op jit(solution)/shard_map/while
  188.6 3.0 %copy-start.6 = (bf16[2,512,8,64]{1,3,2,0:T(8,128)(2,1)S(1)}, bf16[2,512,8,64]{1,3,2,0:T(8,128)(2,1)}, u32[]{:S(2)}) copy-start(bf16[2,512,8,64]{1,3,2,0:T(8,128)(2,1)} %get-tuple-element.343) | copy-start | bytes 3145732 | tf_op jit(solution)/shard_map/while/body/eval_jaxpr/cond
  193.5 4.9 %copy-start.3 = (bf16[2,512,512]{1,2,0:T(8,128)(2,1)S(1)}, bf16[2,512,512]{1,2,0:T(8,128)(2,1)}, u32[]{:S(2)}) copy-start(bf16[2,512,512]{1,2,0:T(8,128)(2,1)} %get-tuple-element.526) | copy-start | bytes 3145732 | tf_op jit(solution)/shard_map/while
  193.5 3.0 %copy-start.4 = (bf16[2,512,8,64]{1,3,2,0:T(8,128)(2,1)S(1)}, bf16[2,512,8,64]{1,3,2,0:T(8,128)(2,1)}, u32[]{:S(2)}) copy-start(bf16[2,512,8,64]{1,3,2,0:T(8,128)(2,1)} %get-tuple-element.353) | copy-start | bytes 3145732 | tf_op jit(solution)/shard_map/while/body/eval_jaxpr/cond
  202.2 4.9 %copy-start.1 = (bf16[2,512,512]{1,2,0:T(8,128)(2,1)S(1)}, bf16[2,512,512]{1,2,0:T(8,128)(2,1)}, u32[]{:S(2)}) copy-start(bf16[2,512,512]{1,2,0:T(8,128)(2,1)} %copy-done) | copy-start | bytes 3145732 | tf_op jit(solution)/shard_map/while
  202.2 3.0 %copy-start.2 = (bf16[2,512,8,64]{1,3,2,0:T(8,128)(2,1)S(1)}, bf16[2,512,8,64]{1,3,2,0:T(8,128)(2,1)}, u32[]{:S(2)}) copy-start(bf16[2,512,8,64]{1,3,2,0:T(8,128)(2,1)} %get-tuple-element.363) | copy-start | bytes 3145732 | tf_op jit(solution)/shard_map/while/body/eval_jaxpr/cond
  219.0 15.3 %copy-start = (bf16[2,512,512]{1,2,0:T(8,128)(2,1)}, bf16[2,512,512]{1,2,0:T(8,128)(2,1)S(1)}, u32[]{:S(2)}) copy-start(bf16[2,512,512]{1,2,0:T(8,128)(2,1)S(1)} %get-tuple-element.528) | copy-start | bytes 3145732 | tf_op jit(solution)/shard_map/while
  237.9 4.9 %copy-start.5 = (bf16[2,512,512]{1,2,0:T(8,128)(2,1)S(1)}, bf16[2,512,512]{1,2,0:T(8,128)(2,1)}, u32[]{:S(2)}) copy-start(bf16[2,512,512]{1,2,0:T(8,128)(2,1)} %get-tuple-element.524) | copy-start | bytes 3145732 | tf_op jit(solution)/shard_map/while
  237.9 3.0 %copy-start.6 = (bf16[2,512,8,64]{1,3,2,0:T(8,128)(2,1)S(1)}, bf16[2,512,8,64]{1,3,2,0:T(8,128)(2,1)}, u32[]{:S(2)}) copy-start(bf16[2,512,8,64]{1,3,2,0:T(8,128)(2,1)} %get-tuple-element.343) | copy-start | bytes 3145732 | tf_op jit(solution)/shard_map/while/body/eval_jaxpr/cond
  246.6 4.9 %copy-start.3 = (bf16[2,512,512]{1,2,0:T(8,128)(2,1)S(1)}, bf16[2,512,512]{1,2,0:T(8,128)(2,1)}, u32[]{:S(2)}) copy-start(bf16[2,512,512]{1,2,0:T(8,128)(2,1)} %get-tuple-element.526) | copy-start | bytes 3145732 | tf_op jit(solution)/shard_map/while
  246.7 3.0 %copy-start.4 = (bf16[2,512,8,64]{1,3,2,0:T(8,128)(2,1)S(1)}, bf16[2,512,8,64]{1,3,2,0:T(8,128)(2,1)}, u32[]{:S(2)}) copy-start(bf16[2,512,8,64]{1,3,2,0:T(8,128)(2,1)} %get-tuple-element.353) | copy-start | bytes 3145732 | tf_op jit(solution)/shard_map/while/body/eval_jaxpr/cond
  251.5 1.2 copy-start.1
where the time goes:
time: 275 us; the launch traced here: 274 us
  waiting for transfers between devices  104 us (38%)
  matrix products  58.5 us (21%)
  local copies, waits for them, and re-layouts  57.8 us (21%)
  starting transfers between devices  22.2 us (8%)
  blocking collectives  17.9 us (7%)
  loops' own time  11.2 us (4%)
    ppermute x4, waiting for transfers between devices, from_behind(): return lax.ppermute(x, axis, pairs)  64.2 us
    dot_general x18, matrix products, block_scores(): jnp.einsum('qhd,khd->hqk', query_tile, kv_block[0], preferred_element_typ...  42.2 us
    all_to_all x1, blocking collectives, shards(): lax.all_to_all(attended, ('head', 'rep'), split_axis=0, concat_axis=1, ti...  17.9 us
    unnamed x10, local copies, waits for them, and re-layouts  16 us
    dot_general x9, matrix products, add_weights(): jnp.einsum('hqk,khd->qhd', rounded, value_block, preferred_element_type=j...  15.7 us
    all_to_all x1, waiting for transfers between devices, shards(): lax.all_to_all(values, ('head', 'rep'), split_axis=1, concat_axis=0, tile...  13.8 us
    all_to_all x1, waiting for transfers between devices, shards(): lax.all_to_all(queries, ('head', 'rep'), split_axis=1, concat_axis=0, til...  13.8 us
    while x1, local copies, waits for them, and re-layouts, shards(): tiles_out = lax.map(attend_tile, jnp.arange(tile_count, dtype=jnp.int32))  13.8 us
  transfers between devices with their start and end apart: 7, of which 5 were waited for; matrix products, arithmetic and copies ran while one was open for 6% of the time, Pallas kernels for 0%

commit v1 on v0

--- a/solution.py
+++ b/solution.py
@@ -1,12 +1,24 @@
+import functools
 import math
 import jax
 import jax.numpy as jnp
 from jax import lax
 from jax.sharding import PartitionSpec as P
+from jax.lax import all_to_all, axis_size
 
 HEAD_DIM = 64
 BLOCK = 512
 REACH = 3
+
+
+def spread_the_cubes(patch, axis_id):
+    return jnp.concatenate(
+        all_to_all(jnp.stack(jnp.split(patch, axis_size(axis_id), axis=0), axis=0), axis_id, 0, 0),
+        axis=1,
+    )
+
+
+manage_ways = functools.partial(spread_the_cubes, axis_id=("head", "rep"))
 
 
 def from_behind(x, axis, by):
@@ -113,7 +125,7 @@
 
     tiles_out = lax.map(attend_tile, jnp.arange(tile_count, dtype=jnp.int32))
     attended = tiles_out.reshape(row_count, feat_width)
-    return lax.all_to_all(attended, ("head", "rep"), split_axis=0, concat_axis=1, tiled=True)
+    return manage_ways(attended)
 
 
 def solution(mesh):

time: 275 us -> 276 us (level)
  no operation moved by 1% of the time
where the time goes in v1:
time: 276 us; the launch traced here: 274 us
  waiting for transfers between devices  104 us (38%)
  local copies, waits for them, and re-layouts  59.4 us (22%)
  matrix products  58.5 us (21%)
  starting transfers between devices  22.2 us (8%)
  blocking collectives  16.9 us (6%)
  loops' own time  11.2 us (4%)
    ppermute x4, waiting for transfers between devices, from_behind(): return lax.ppermute(x, axis, pairs)  64.2 us
    dot_general x18, matrix products, block_scores(): jnp.einsum('qhd,khd->hqk', query_tile, kv_block[0], preferred_element_typ...  42.2 us
    all_to_all x1, blocking collectives, spread_the_cubes(): all_to_all(jnp.stack(jnp.split(patch, axis_size(axis_id), axis=0), axis=0...  16.9 us
    unnamed x10, local copies, waits for them, and re-layouts  16.1 us
    dot_general x9, matrix products, add_weights(): jnp.einsum('hqk,khd->qhd', rounded, value_block, preferred_element_type=j...  15.7 us
    while x1, local copies, waits for them, and re-layouts, shards(): tiles_out = lax.map(attend_tile, jnp.arange(tile_count, dtype=jnp.int32))  13.9 us
    all_to_all x1, waiting for transfers between devices, shards(): lax.all_to_all(values, ('head', 'rep'), split_axis=1, concat_axis=0, tile...  13.8 us
    all_to_all x1, waiting for transfers between devices, shards(): lax.all_to_all(queries, ('head', 'rep'), split_axis=1, concat_axis=0, til...  13.8 us
  transfers between devices with their start and end apart: 7, of which 5 were waited for; matrix products, arithmetic and copies ran while one was open for 6% of the time, Pallas kernels for 0%

profile of v1, /device:TPU:20, one launch (start us, length us, event | category | flops | bytes accessed | tf_op | source)
XLA Modules:
  0.0 274.4 jit_solution(11825394490094843431)
XLA Ops:
  0.0 2.3 copy.63
  2.3 3.5 %all-to-all-start = ((bf16[256,4,512]{0,2,1:T(8,128)(2,1)}), bf16[256,4,512]{0,2,1:T(8,128)(2,1)S(1)}, u32[]{:S(2)}, u32[]{:S(2)}) async-start(bf16[256,4,512]{0,2,1:T(8,128)(2,1)} %bitcast.46), calls=%async_computation | async-start | bytes 2097152 | tf_op jit(solution)/shard_map/all_to_all | solution.py:33
  5.8 2.3 copy.65
  8.1 12.1 %all-to-all-done = bf16[256,4,512]{0,2,1:T(8,128)(2,1)S(1)} async-done(((bf16[256,4,512]{0,2,1:T(8,128)(2,1)}), bf16[256,4,512]{0,2,1:T(8,128)(2,1)S(1)}, u32[]{:S(2)}, u32[]{:S(2)}) %all-to-all-start) | async-done | bytes 1048608 | tf_op jit(solution)/shard_map/all_to_all | solution.py:33
  20.2 3.5 %all-to-all-start.1 = ((bf16[256,4,512]{0,2,1:T(8,128)(2,1)}), bf16[256,4,512]{0,2,1:T(8,128)(2,1)S(1)}, u32[]{:S(2)}, u32[]{:S(2)}) async-start(bf16[256,4,512]{0,2,1:T(8,128)(2,1)} %bitcast.49), calls=%async_computation.1 | async-start | bytes 2097152 | tf_op jit(solution)/shard_map/all_to_all | solution.py:34
  24.3 13.8 %all-to-all-done.1 = bf16[256,4,512]{0,2,1:T(8,128)(2,1)S(1)} async-done(((bf16[256,4,512]{0,2,1:T(8,128)(2,1)}), bf16[256,4,512]{0,2,1:T(8,128)(2,1)S(1)}, u32[]{:S(2)}, u32[]{:S(2)}) %all-to-all-start.1) | async-done | bytes 1048608 | tf_op jit(solution)/shard_map/all_to_all | solution.py:34
  38.9 3.5 %collective-permute-start = (bf16[2,1024,512]{2,1,0:T(8,128)(2,1)S(1)}, bf16[2,1024,512]{2,1,0:T(8,128)(2,1)}, u32[]{:S(2)}, u32[]{:S(2)}) collective-permute-start(bf16[2,1024,512]{2,1,0:T(8,128)(2,1)S(1)} %pad_maximum_fusion), channel_id=1, source_target_pairs={{0,4},{4,8},{8,12},{1,5},{5,9},{9,13},{2,6},{6,10},{10,14},{3,7},{... | collective-permute-start | bytes 6291464 | tf_op jit(solution)/shard_map/ppermute | solution.py:27
  42.3 2.4 collective-permute-start.2
  44.7 43.2 %collective-permute-done = bf16[2,1024,512]{2,1,0:T(8,128)(2,1)} collective-permute-done((bf16[2,1024,512]{2,1,0:T(8,128)(2,1)S(1)}, bf16[2,1024,512]{2,1,0:T(8,128)(2,1)}, u32[]{:S(2)}, u32[]{:S(2)}) %collective-permute-start) | collective-permute-done | bytes 2097184 | tf_op jit(solution)/shard_map/ppermute | solution.py:27
  87.9 3.5 %collective-permute-start.1 = (bf16[2,1024,512]{2,1,0:T(8,128)(2,1)}, bf16[2,1024,512]{2,1,0:T(8,128)(2,1)}, u32[]{:S(2)}, u32[]{:S(2)}) collective-permute-start(bf16[2,1024,512]{2,1,0:T(8,128)(2,1)} %collective-permute-done), channel_id=1, source_target_pairs={{0,4},{4,8},{8,12},{1,5},{5,9},{9,13},{2,6},{6,10},{10,14},{3,7},{... | collective-permute-start | bytes 6291464 | tf_op jit(solution)/shard_map/ppermute | solution.py:27
  91.4 2.4 collective-permute-start.3
  93.8 2.3 copy.67
  96.1 3.5 %all-to-all-start.2 = ((bf16[256,4,512]{0,2,1:T(8,128)(2,1)}), bf16[256,4,512]{0,2,1:T(8,128)(2,1)S(1)}, u32[]{:S(2)}, u32[]{:S(2)}) async-start(bf16[256,4,512]{0,2,1:T(8,128)(2,1)} %bitcast.230), calls=%async_computation.2 | async-start | bytes 2097152 | tf_op jit(solution)/shard_map/all_to_all | solution.py:32
  100.2 13.8 %all-to-all-done.2 = bf16[256,4,512]{0,2,1:T(8,128)(2,1)S(1)} async-done(((bf16[256,4,512]{0,2,1:T(8,128)(2,1)}), bf16[256,4,512]{0,2,1:T(8,128)(2,1)S(1)}, u32[]{:S(2)}, u32[]{:S(2)}) %all-to-all-start.2) | async-done | bytes 1048608 | tf_op jit(solution)/shard_map/all_to_all | solution.py:32
  115.3 21.0 %collective-permute-done.1 = bf16[2,1024,512]{2,1,0:T(8,128)(2,1)} collective-permute-done((bf16[2,1024,512]{2,1,0:T(8,128)(2,1)}, bf16[2,1024,512]{2,1,0:T(8,128)(2,1)}, u32[]{:S(2)}, u32[]{:S(2)}) %collective-permute-start.1) | collective-permute-done | bytes 2097184 | tf_op jit(solution)/shard_map/ppermute | solution.py:27
  136.3 3.0 %constant_dynamic-update-slice_fusion.5 = bf16[2,5120,512]{2,1,0:T(8,128)(2,1)} fusion(bf16[2,1024,512]{2,1,0:T(8,128)(2,1)} %collective-permute-done.1), kind=kLoop, calls=%fused_computation.138 | loop fusion | bytes 4194304
  139.4 3.1 %constant_dynamic-update-slice_fusion.4 = bf16[2,5120,512]{2,1,0:T(8,128)(2,1)} fusion(bf16[2,5120,512]{2,1,0:T(8,128)(2,1)} %constant_dynamic-update-slice_fusion.5, bf16[2,1024,512]{2,1,0:T(8,128)(2,1)} %collective-permute-done), kind=kLoop, calls=%fused_computation.137 | loop fusion | bytes 4194304
  144.0 3.0 %constant_dynamic-update-slice_fusion.2 = bf16[2,5120,512]{2,1,0:T(8,128)(2,1)} fusion(bf16[2,5120,512]{2,1,0:T(8,128)(2,1)} %constant_dynamic-update-slice_fusion.3, bf16[2,1024,512]{2,1,0:T(8,128)(2,1)} %collective-permute-done.2), kind=kLoop, calls=%fused_computation.135 | loop fusion | bytes 4194304
  147.0 3.1 %constant_dynamic-update-slice_fusion.1 = bf16[2,5120,512]{2,1,0:T(8,128)(2,1)} fusion(bf16[2,5120,512]{2,1,0:T(8,128)(2,1)} %constant_dynamic-update-slice_fusion.2, bf16[2,1024,512]{2,1,0:T(8,128)(2,1)} %collective-permute-done.3), kind=kLoop, calls=%fused_computation.134 | loop fusion | bytes 4194304 | tf_op jit(solution)/shard_map/concatenate | solution.py:52
  150.1 13.9 %copy.69 = bf16[2,5120,512]{1,2,0:T(8,128)(2,1)} copy(bf16[2,5120,512]{2,1,0:T(8,128)(2,1)} %constant_dynamic-update-slice_fusion.1) | data formatting | bytes 20971520 | tf_op jit(solution)/shard_map/while | solution.py:126
  164.0 90.1 %while.13 = (s32[]{:T(128)}, bf16[2,512,512]{2,1,0:T(8,128)(2,1)}, s32[2]{0:T(128)S(1)}, s32[]{:T(128)}, f32[14,8]{0,1:T(8,128)S(1)}, /*index=5*/bf16[2,5120,512...) while((s32[]{:T(128)}, bf16[2,512,512]{2,1,0:T(8,128)(2,1)}, ...), condition=%wide.region_43.44_spmd, body=%wide.region_0.43_spmd.sunk | while | flops 5756674048 | bytes 200296880 | solution.py:126
  165.4 5.6 %constant_dynamic-slice_fusion.10 = (bf16[2,512,512]{1,2,0:T(8,128)(2,1)S(1)}, bf16[2,512,512]{1,2,0:T(8,128)(2,1)}, bf16[2,512,512]{1,2,0:T(8,128)(2,1)}, bf16[...) fusion(bf16[2,5120,512]{1,2,0:T(8,128)(2,1)} %get-tuple-element, ...), kind=kLoop, calls=%fused_computation.120.clone.1 | loop fusion | bytes 14680092 | tf_op jit(solution)/shard_map/while/body/eval_jaxpr/dynamic_slice | solution.py:76
  174.6 2.4 conditional.29
  174.6 2.3 multiply_reduce_fusion.1
  178.3 2.4 conditional.31
  178.3 2.3 multiply_reduce_fusion.3
  181.2 2.4 conditional.32
  181.2 2.3 multiply_reduce_fusion.4
  184.3 2.4 conditional.33
  184.3 2.3 multiply_reduce_fusion.5
  188.8 4.8 %conditional.36 = ((f32[512,8,64]{0,2,1:T(8,128)S(1)}, f32[8,512]{1,0:T(8,128)S(1)})) conditional(s32[]{:T(128)} %bitcast.183, (f32[512,8,64]{0,2,1:T(8,128)S(1)}, f32[8,512]{1,0:T(8,128)S(1)}) %conditional.35, (bf16[2,512,8,64]{1,3,2,0:T(8,128)(2,1)}, bf16[512,8,64]{0,2,1:T(8,128)(2,1)S(1)}, f32[8,512]{1,0:T(8,128)S(1)}, ...), branch_computations={%region_25.25_spmd, %region_26.27_spmd} | conditional | flops 549715968 | bytes 24739892 | solution.py:115
  188.8 3.0 %fusion.29 = (f32[8,512]{1,0:T(8,128)S(1)}, f32[8,512,512]{1,2,0:T(8,128)S(1)}) fusion(f32[8,512]{1,0:T(8,128)S(1)} %get-tuple-element.344, bf16[512,8,64]{0,2,1:T(8,128)(2,1)S(1)} %get-tuple-element.342, bf16[2,512,8,64]{1,3,2,0:T(8,128)(2,1)} %get-tuple-element.343), kind=kOutput, calls=%fused_computation.35 | convolution fusion | flops 274722816 | bytes 9469952 | tf_op jit(solution)/shard_map/while/body/eval_jaxpr/cond/branch_1_fun/qhd,khd->hqk/dot_general | solution.py:81
  191.8 1.8 fusion.38
  193.7 4.8 %conditional.38 = ((f32[512,8,64]{0,2,1:T(8,128)S(1)}, f32[8,512]{1,0:T(8,128)S(1)})) conditional(s32[]{:T(128)} %bitcast.181, (f32[512,8,64]{0,2,1:T(8,128)S(1)}, f32[8,512]{1,0:T(8,128)S(1)}) %get-tuple-element.658, (bf16[2,512,8,64]{1,3,2,0:T(8,128)(2,1)}, bf16[512,8,64]{0,2,1:T(8,128)(2,1)S(1)}, f32[8,512]{1,0:T(8,128)S(1)}, ...), branch_computations={%region_31.31_spmd, %region_32.33_spmd} | conditional | flops 549715968 | bytes 24739892 | solution.py:115
  193.7 3.0 %fusion.65 = (f32[8,512]{1,0:T(8,128)S(1)}, f32[8,512,512]{1,2,0:T(8,128)S(1)}) fusion(f32[8,512]{1,0:T(8,128)S(1)} %get-tuple-element.354, bf16[512,8,64]{0,2,1:T(8,128)(2,1)S(1)} %get-tuple-element.352, bf16[2,512,8,64]{1,3,2,0:T(8,128)(2,1)} %get-tuple-element.353), kind=kOutput, calls=%fused_computation.63 | convolution fusion | flops 274722816 | bytes 9469952 | tf_op jit(solution)/shard_map/while/body/eval_jaxpr/cond/branch_1_fun/qhd,khd->hqk/dot_general | solution.py:81
  196.7 1.8 fusion.74
  198.5 3.9 %conditional.39 = ((f32[512,8,64]{0,2,1:T(8,128)S(1)}, f32[8,512]{1,0:T(8,128)S(1)})) conditional(s32[]{:T(128)} %bitcast.180, (f32[512,8,64]{0,2,1:T(8,128)S(1)}, f32[8,512]{1,0:T(8,128)S(1)}) %get-tuple-element.659, (bf16[2,512,8,64]{1,3,2,0:T(8,128)(2,1)S(1)}, bf16[512,8,64]{0,2,1:T(8,128)(2,1)S(1)}, f32[8,512]{1,0:T(8,128)S(1)}, ...), branch_computations={%region_34.34_spmd, %region_35.36_spmd} | conditional | flops 549715968 | bytes 20545560 | solution.py:115
  198.5 2.0 fusion.83
  200.6 1.8 fusion.92
  202.4 4.8 %conditional.40 = ((f32[512,8,64]{0,2,1:T(8,128)S(1)}, f32[8,512]{1,0:T(8,128)S(1)})) conditional(s32[]{:T(128)} %bitcast.179, (f32[512,8,64]{0,2,1:T(8,128)S(1)}, f32[8,512]{1,0:T(8,128)S(1)}) %get-tuple-element.660, (bf16[2,512,8,64]{1,3,2,0:T(8,128)(2,1)}, bf16[512,8,64]{0,2,1:T(8,128)(2,1)S(1)}, f32[8,512]{1,0:T(8,128)S(1)}, ...), branch_computations={%region_37.37_spmd, %region_38.39_spmd} | conditional | flops 549715968 | bytes 24739892 | solution.py:115
  202.4 3.0 %fusion.101 = (f32[8,512]{1,0:T(8,128)S(1)}, f32[8,512,512]{1,2,0:T(8,128)S(1)}) fusion(f32[8,512]{1,0:T(8,128)S(1)} %get-tuple-element.364, bf16[512,8,64]{0,2,1:T(8,128)(2,1)S(1)} %get-tuple-element.362, bf16[2,512,8,64]{1,3,2,0:T(8,128)(2,1)} %get-tuple-element.363), kind=kOutput, calls=%fused_computation.91 | convolution fusion | flops 274722816 | bytes 9469952 | tf_op jit(solution)/shard_map/while/body/eval_jaxpr/cond/branch_1_fun/qhd,khd->hqk/dot_general | solution.py:81
  205.4 1.8 fusion.110
  207.2 3.9 %conditional.41 = ((f32[512,8,64]{0,2,1:T(8,128)S(1)}, f32[8,512]{1,0:T(8,128)S(1)})) conditional(s32[]{:T(128)} %bitcast.178, (f32[512,8,64]{0,2,1:T(8,128)S(1)}, f32[8,512]{1,0:T(8,128)S(1)}) %get-tuple-element.661, (bf16[2,512,8,64]{1,3,2,0:T(8,128)(2,1)S(1)}, bf16[512,8,64]{0,2,1:T(8,128)(2,1)S(1)}, f32[8,512]{1,0:T(8,128)S(1)}, ...), branch_computations={%region_40.40_spmd, %region_41.42_spmd} | conditional | flops 549715968 | bytes 20545560 | solution.py:115
  207.3 2.0 fusion.119
  209.3 1.8 fusion.128
  213.6 5.6 %constant_dynamic-slice_fusion.10 = (bf16[2,512,512]{1,2,0:T(8,128)(2,1)S(1)}, bf16[2,512,512]{1,2,0:T(8,128)(2,1)}, bf16[2,512,512]{1,2,0:T(8,128)(2,1)}, bf16[...) fusion(bf16[2,5120,512]{1,2,0:T(8,128)(2,1)} %get-tuple-element, ...), kind=kLoop, calls=%fused_computation.120.clone.1 | loop fusion | bytes 14680092 | tf_op jit(solution)/shard_map/while/body/eval_jaxpr/dynamic_slice | solution.py:76
  224.2 2.4 conditional.29
  224.2 2.3 multiply_reduce_fusion.1
  227.3 2.4 conditional.30
  227.3 2.3 multiply_reduce_fusion.2
  230.2 2.4 conditional.31
  230.2 2.3 multiply_reduce_fusion.3
  234.5 3.6 %conditional.35 = (f32[512,8,64]{0,2,1:T(8,128)S(1)}, f32[8,512]{1,0:T(8,128)S(1)}) conditional(s32[]{:T(128)} %bitcast.184, () %tuple.158, (bf16[2,512,8,64]{1,3,2,0:T(8,128)(2,1)S(1)}, bf16[512,8,64]{0,2,1:T(8,128)(2,1)S(1)}, f32[8,512]{1,0:T(8,128)S(1)}) %tuple.232), branch_computations={%region_22.22_spmd, %region_23.24_spmd} | conditional | flops 549449728 | bytes 19447824 | solution.py:115
  234.5 2.0 fusion.14
  238.2 4.8 %conditional.36 = ((f32[512,8,64]{0,2,1:T(8,128)S(1)}, f32[8,512]{1,0:T(8,128)S(1)})) conditional(s32[]{:T(128)} %bitcast.183, (f32[512,8,64]{0,2,1:T(8,128)S(1)}, f32[8,512]{1,0:T(8,128)S(1)}) %conditional.35, (bf16[2,512,8,64]{1,3,2,0:T(8,128)(2,1)}, bf16[512,8,64]{0,2,1:T(8,128)(2,1)S(1)}, f32[8,512]{1,0:T(8,128)S(1)}, ...), branch_computations={%region_25.25_spmd, %region_26.27_spmd} | conditional | flops 549715968 | bytes 24739892 | solution.py:115
  238.2 3.0 %fusion.29 = (f32[8,512]{1,0:T(8,128)S(1)}, f32[8,512,512]{1,2,0:T(8,128)S(1)}) fusion(f32[8,512]{1,0:T(8,128)S(1)} %get-tuple-element.344, bf16[512,8,64]{0,2,1:T(8,128)(2,1)S(1)} %get-tuple-element.342, bf16[2,512,8,64]{1,3,2,0:T(8,128)(2,1)} %get-tuple-element.343), kind=kOutput, calls=%fused_computation.35 | convolution fusion | flops 274722816 | bytes 9469952 | tf_op jit(solution)/shard_map/while/body/eval_jaxpr/cond/branch_1_fun/qhd,khd->hqk/dot_general | solution.py:81
  241.2 1.8 fusion.38
  243.0 3.9 %conditional.37 = ((f32[512,8,64]{0,2,1:T(8,128)S(1)}, f32[8,512]{1,0:T(8,128)S(1)})) conditional(s32[]{:T(128)} %bitcast.182, (f32[512,8,64]{0,2,1:T(8,128)S(1)}, f32[8,512]{1,0:T(8,128)S(1)}) %get-tuple-element.657, (bf16[2,512,8,64]{1,3,2,0:T(8,128)(2,1)S(1)}, bf16[512,8,64]{0,2,1:T(8,128)(2,1)S(1)}, f32[8,512]{1,0:T(8,128)S(1)}, ...), branch_computations={%region_28.28_spmd, %region_29.30_spmd} | conditional | flops 549715968 | bytes 20545560 | solution.py:115
  243.0 2.0 fusion.47
  245.1 1.8 fusion.56
  246.9 4.8 %conditional.38 = ((f32[512,8,64]{0,2,1:T(8,128)S(1)}, f32[8,512]{1,0:T(8,128)S(1)})) conditional(s32[]{:T(128)} %bitcast.181, (f32[512,8,64]{0,2,1:T(8,128)S(1)}, f32[8,512]{1,0:T(8,128)S(1)}) %get-tuple-element.658, (bf16[2,512,8,64]{1,3,2,0:T(8,128)(2,1)}, bf16[512,8,64]{0,2,1:T(8,128)(2,1)S(1)}, f32[8,512]{1,0:T(8,128)S(1)}, ...), branch_computations={%region_31.31_spmd, %region_32.33_spmd} | conditional | flops 549715968 | bytes 24739892 | solution.py:115
  246.9 3.0 %fusion.65 = (f32[8,512]{1,0:T(8,128)S(1)}, f32[8,512,512]{1,2,0:T(8,128)S(1)}) fusion(f32[8,512]{1,0:T(8,128)S(1)} %get-tuple-element.354, bf16[512,8,64]{0,2,1:T(8,128)(2,1)S(1)} %get-tuple-element.352, bf16[2,512,8,64]{1,3,2,0:T(8,128)(2,1)} %get-tuple-element.353), kind=kOutput, calls=%fused_computation.63 | convolution fusion | flops 274722816 | bytes 9469952 | tf_op jit(solution)/shard_map/while/body/eval_jaxpr/cond/branch_1_fun/qhd,khd->hqk/dot_general | solution.py:81
  249.9 1.8 fusion.74
  255.6 16.9 %all_to_all.56 = bf16[4,256,512]{2,1,0:T(8,128)(2,1)S(1)} all-to-all(bf16[4,256,512]{2,1,0:T(8,128)(2,1)S(1)} %pad_maximum_fusion.1), channel_id=1, replica_groups=mesh['grp'=2,'ctx'=4,'head'=2,'rep'=2] {'head','rep'}, dimensions={0} | all-to-all | bytes 2097152 | tf_op jit(solution)/shard_map/all_to_all | solution.py:16
  (96 shorter events, 25.0 us)
Async XLA Ops:
  2.3 17.9 %all-to-all-start = ((bf16[256,4,512]{0,2,1:T(8,128)(2,1)}), bf16[256,4,512]{0,2,1:T(8,128)(2,1)S(1)}, u32[]{:S(2)}, u32[]{:S(2)}) async-start(bf16[256,4,512]{0,2,1:T(8,128)(2,1)} %bitcast.46), calls=%async_computation | async-start | bytes 2097152 | tf_op jit(solution)/shard_map/all_to_all | solution.py:33
  5.8 93.9 %copy-start.7 = (s32[8,8]{1,0:T(8,128)S(1)}, s32[8,8]{1,0:T(8,128)}, u32[]{:S(2)}) copy-start(s32[8,8]{1,0:T(8,128)} %param.38) | copy-start | bytes 772
  5.8 93.9 %copy-start.8 = (s32[8]{0:T(128)S(1)}, s32[8]{0:T(128)}, u32[]{:S(2)}) copy-start(s32[8]{0:T(128)} %param.39) | copy-start | bytes 100
  20.2 17.9 %all-to-all-start.1 = ((bf16[256,4,512]{0,2,1:T(8,128)(2,1)}), bf16[256,4,512]{0,2,1:T(8,128)(2,1)S(1)}, u32[]{:S(2)}, u32[]{:S(2)}) async-start(bf16[256,4,512]{0,2,1:T(8,128)(2,1)} %bitcast.49), calls=%async_computation.1 | async-start | bytes 2097152 | tf_op jit(solution)/shard_map/all_to_all | solution.py:34
  38.9 49.1 %collective-permute-start = (bf16[2,1024,512]{2,1,0:T(8,128)(2,1)S(1)}, bf16[2,1024,512]{2,1,0:T(8,128)(2,1)}, u32[]{:S(2)}, u32[]{:S(2)}) collective-permute-start(bf16[2,1024,512]{2,1,0:T(8,128)(2,1)S(1)} %pad_maximum_fusion), channel_id=1, source_target_pairs={{0,4},{4,8},{8,12},{1,5},{5,9},{9,13},{2,6},{6,10},{10,14},{3,7},{... | collective-permute-start | bytes 6291464 | tf_op jit(solution)/shard_map/ppermute | solution.py:27
  42.3 49.1 %collective-permute-start.2 = (bf16[2,1024,512]{2,1,0:T(8,128)(2,1)S(1)}, bf16[2,1024,512]{2,1,0:T(8,128)(2,1)}, u32[]{:S(2)}, u32[]{:S(2)}) collective-permute-start(bf16[2,1024,512]{2,1,0:T(8,128)(2,1)S(1)} %pad_maximum_fusion), channel_id=1, source_target_pairs={{4,0},{8,4},{12,8},{5,1},{9,5},{13,9},{6,2},{10,6},{14,10},{7,3},{... | collective-permute-start | bytes 6291464 | tf_op jit(solution)/shard_map/ppermute | solution.py:27
  87.9 48.4 %collective-permute-start.1 = (bf16[2,1024,512]{2,1,0:T(8,128)(2,1)}, bf16[2,1024,512]{2,1,0:T(8,128)(2,1)}, u32[]{:S(2)}, u32[]{:S(2)}) collective-permute-start(bf16[2,1024,512]{2,1,0:T(8,128)(2,1)} %collective-permute-done), channel_id=1, source_target_pairs={{0,4},{4,8},{8,12},{1,5},{5,9},{9,13},{2,6},{6,10},{10,14},{3,7},{... | collective-permute-start | bytes 6291464 | tf_op jit(solution)/shard_map/ppermute | solution.py:27
  91.4 55.6 %collective-permute-start.3 = (bf16[2,1024,512]{2,1,0:T(8,128)(2,1)}, bf16[2,1024,512]{2,1,0:T(8,128)(2,1)}, u32[]{:S(2)}, u32[]{:S(2)}) collective-permute-start(bf16[2,1024,512]{2,1,0:T(8,128)(2,1)} %collective-permute-done.2), channel_id=1, source_target_pairs={{4,0},{8,4},{12,8},{5,1},{9,5},{13,9},{6,2},{10,6},{14,10},{7,3},{... | collective-permute-start | bytes 6291464 | tf_op jit(solution)/shard_map/ppermute | solution.py:27
  96.1 17.9 %all-to-all-start.2 = ((bf16[256,4,512]{0,2,1:T(8,128)(2,1)}), bf16[256,4,512]{0,2,1:T(8,128)(2,1)S(1)}, u32[]{:S(2)}, u32[]{:S(2)}) async-start(bf16[256,4,512]{0,2,1:T(8,128)(2,1)} %bitcast.230), calls=%async_computation.2 | async-start | bytes 2097152 | tf_op jit(solution)/shard_map/all_to_all | solution.py:32
  170.9 16.3 %copy-start = (bf16[2,512,512]{1,2,0:T(8,128)(2,1)}, bf16[2,512,512]{1,2,0:T(8,128)(2,1)S(1)}, u32[]{:S(2)}) copy-start(bf16[2,512,512]{1,2,0:T(8,128)(2,1)S(1)} %get-tuple-element.532) | copy-start | bytes 3145732 | tf_op jit(solution)/shard_map/while
  188.8 4.9 %copy-start.5 = (bf16[2,512,512]{1,2,0:T(8,128)(2,1)S(1)}, bf16[2,512,512]{1,2,0:T(8,128)(2,1)}, u32[]{:S(2)}) copy-start(bf16[2,512,512]{1,2,0:T(8,128)(2,1)} %get-tuple-element.528) | copy-start | bytes 3145732 | tf_op jit(solution)/shard_map/while
  188.8 3.0 %copy-start.6 = (bf16[2,512,8,64]{1,3,2,0:T(8,128)(2,1)S(1)}, bf16[2,512,8,64]{1,3,2,0:T(8,128)(2,1)}, u32[]{:S(2)}) copy-start(bf16[2,512,8,64]{1,3,2,0:T(8,128)(2,1)} %get-tuple-element.343) | copy-start | bytes 3145732 | tf_op jit(solution)/shard_map/while/body/eval_jaxpr/cond
  193.7 4.9 %copy-start.3 = (bf16[2,512,512]{1,2,0:T(8,128)(2,1)S(1)}, bf16[2,512,512]{1,2,0:T(8,128)(2,1)}, u32[]{:S(2)}) copy-start(bf16[2,512,512]{1,2,0:T(8,128)(2,1)} %get-tuple-element.530) | copy-start | bytes 3145732 | tf_op jit(solution)/shard_map/while
  193.7 3.0 %copy-start.4 = (bf16[2,512,8,64]{1,3,2,0:T(8,128)(2,1)S(1)}, bf16[2,512,8,64]{1,3,2,0:T(8,128)(2,1)}, u32[]{:S(2)}) copy-start(bf16[2,512,8,64]{1,3,2,0:T(8,128)(2,1)} %get-tuple-element.353) | copy-start | bytes 3145732 | tf_op jit(solution)/shard_map/while/body/eval_jaxpr/cond
  202.4 4.9 %copy-start.1 = (bf16[2,512,512]{1,2,0:T(8,128)(2,1)S(1)}, bf16[2,512,512]{1,2,0:T(8,128)(2,1)}, u32[]{:S(2)}) copy-start(bf16[2,512,512]{1,2,0:T(8,128)(2,1)} %copy-done) | copy-start | bytes 3145732 | tf_op jit(solution)/shard_map/while
  202.4 3.0 %copy-start.2 = (bf16[2,512,8,64]{1,3,2,0:T(8,128)(2,1)S(1)}, bf16[2,512,8,64]{1,3,2,0:T(8,128)(2,1)}, u32[]{:S(2)}) copy-start(bf16[2,512,8,64]{1,3,2,0:T(8,128)(2,1)} %get-tuple-element.363) | copy-start | bytes 3145732 | tf_op jit(solution)/shard_map/while/body/eval_jaxpr/cond
  219.2 15.3 %copy-start = (bf16[2,512,512]{1,2,0:T(8,128)(2,1)}, bf16[2,512,512]{1,2,0:T(8,128)(2,1)S(1)}, u32[]{:S(2)}) copy-start(bf16[2,512,512]{1,2,0:T(8,128)(2,1)S(1)} %get-tuple-element.532) | copy-start | bytes 3145732 | tf_op jit(solution)/shard_map/while
  238.1 4.9 %copy-start.5 = (bf16[2,512,512]{1,2,0:T(8,128)(2,1)S(1)}, bf16[2,512,512]{1,2,0:T(8,128)(2,1)}, u32[]{:S(2)}) copy-start(bf16[2,512,512]{1,2,0:T(8,128)(2,1)} %get-tuple-element.528) | copy-start | bytes 3145732 | tf_op jit(solution)/shard_map/while
  238.2 3.0 %copy-start.6 = (bf16[2,512,8,64]{1,3,2,0:T(8,128)(2,1)S(1)}, bf16[2,512,8,64]{1,3,2,0:T(8,128)(2,1)}, u32[]{:S(2)}) copy-start(bf16[2,512,8,64]{1,3,2,0:T(8,128)(2,1)} %get-tuple-element.343) | copy-start | bytes 3145732 | tf_op jit(solution)/shard_map/while/body/eval_jaxpr/cond
  246.9 4.9 %copy-start.3 = (bf16[2,512,512]{1,2,0:T(8,128)(2,1)S(1)}, bf16[2,512,512]{1,2,0:T(8,128)(2,1)}, u32[]{:S(2)}) copy-start(bf16[2,512,512]{1,2,0:T(8,128)(2,1)} %get-tuple-element.530) | copy-start | bytes 3145732 | tf_op jit(solution)/shard_map/while
  246.9 3.0 %copy-start.4 = (bf16[2,512,8,64]{1,3,2,0:T(8,128)(2,1)S(1)}, bf16[2,512,8,64]{1,3,2,0:T(8,128)(2,1)}, u32[]{:S(2)}) copy-start(bf16[2,512,8,64]{1,3,2,0:T(8,128)(2,1)} %get-tuple-element.353) | copy-start | bytes 3145732 | tf_op jit(solution)/shard_map/while/body/eval_jaxpr/cond
  251.7 1.2 copy-start.1
